TPU v7x, 32 devices: a whole 2x2x4 slice. The times are simulated.
32 devices in a mesh: row: 4 (over y, x), col: 4 (over z), depth: 2 (over core).
Axes of the slice: x: 2, y: 2, z: 4, core: 2. Of those that a mesh axis runs over, the one named last changes fastest.
Arguments:
- matrix_panel: bfloat16 [12288, 65536], P('row', 'col'), may hold values from -0.1484375 to 0.1484375
- start_block: bfloat16 [12288, 64], P('row', 'depth'), may hold values from -6 to 6
- stored_basis: float32 [12288, 1024], P('row'), may hold values from -2.2 to 2.2
Outputs:
- new_block: float32 [12288, 64], P('row', 'depth')
- coefficients: float32 [1024, 64], P(None, 'depth')
- triangle: float32 [64, 64], replicated
All inputs are finite; a program needn't handle non-finite values.
Results may differ from a plain program's by a relative error of at most 0.0023.
Values may be sent and summed in bfloat16 or wider, within the bound.
A program may use at most 256 MiB of HBM per device.

v0:
```python
import jax
import jax.numpy as jnp
from jax import lax
from jax.sharding import PartitionSpec as P

HIGHEST = lax.Precision.HIGHEST


def contract_rows(left_side, right_side, mode):
    return lax.dot_general(
        left_side,
        right_side,
        (((0,), (0,)), ((), ())),
        precision=mode,
        preferred_element_type=jnp.float32,
    )


def factor_gram(gram_matrix):
    lower_factor = jnp.linalg.cholesky(gram_matrix)
    identity = jnp.eye(gram_matrix.shape[0], dtype=jnp.float32)
    inverse = jax.scipy.linalg.solve_triangular(lower_factor, identity, lower=True)
    return (lower_factor, inverse)


def orthonormal_pass(stored_basis, block_cols, reduce_sum, row_total):
    projection = reduce_sum(contract_rows(stored_basis, block_cols, HIGHEST)) / row_total
    remainder = block_cols - jnp.dot(
        stored_basis, projection, precision=HIGHEST, preferred_element_type=jnp.float32
    )
    gram_matrix = reduce_sum(contract_rows(remainder, remainder, HIGHEST)) / row_total
    lower_factor, inverse = factor_gram(gram_matrix)
    normed = jnp.dot(remainder, inverse.T, precision=HIGHEST, preferred_element_type=jnp.float32)
    return (projection, lower_factor, normed)


def per_device(matrix_panel, start_block, stored_basis):
    row_total = stored_basis.shape[0] * lax.axis_size("row")
    half_cols = start_block.shape[1]
    depth_index = lax.axis_index("depth")
    whole_start = lax.all_gather(start_block, "depth", axis=1, tiled=True)
    half_rows = matrix_panel.shape[0] // 2
    panel_rows = lax.dynamic_slice_in_dim(matrix_panel, depth_index * half_rows, half_rows, 0)
    start_rows = lax.dynamic_slice_in_dim(whole_start, depth_index * half_rows, half_rows, 0)
    basis_rows = lax.dynamic_slice_in_dim(stored_basis, depth_index * half_rows, half_rows, 0)
    mixed_cols = lax.psum(contract_rows(panel_rows, start_rows, None), ("row", "depth")).astype(
        jnp.bfloat16
    )
    image_block = lax.psum(
        jnp.dot(panel_rows, mixed_cols, preferred_element_type=jnp.float32), "col"
    )

    def sum_layers(value):
        return lax.psum(value, ("row", "depth"))

    proj_first, lower_first, normed_first = orthonormal_pass(
        basis_rows, image_block, sum_layers, row_total
    )
    proj_second, lower_second, normed_second = orthonormal_pass(
        basis_rows, normed_first, sum_layers, row_total
    )
    new_block = lax.all_to_all(normed_second, "depth", split_axis=1, concat_axis=0, tiled=True)
    coef_whole = proj_first + jnp.dot(
        proj_second, lower_first.T, precision=HIGHEST, preferred_element_type=jnp.float32
    )
    coefficients = lax.dynamic_slice_in_dim(coef_whole, depth_index * half_cols, half_cols, 1)
    triangle = jnp.dot(
        lower_second.T, lower_first.T, precision=HIGHEST, preferred_element_type=jnp.float32
    )
    return (new_block, coefficients, triangle)


def solution(mesh):
    placed = (P("row", "col"), P("row", "depth"), P("row", None))
    return jax.shard_map(
        per_device,
        mesh=mesh,
        in_specs=placed,
        out_specs=(P("row", "depth"), P(None, "depth"), P()),
        check_vma=False,
    )
```

profile of v0, /device:TPU:0, one launch (start us, length us, event | category | flops | bytes accessed | tf_op | source)
XLA Modules:
  0.0 405.6 jit_solution(3928022254567349980)
XLA Ops:
  7.2 2.4 all_gather.3
  9.6 20.5 %fusion.2 = f32[16384,64]{0,1:T(8,128)} fusion(bf16[3072,16384]{1,0:T(8,128)(2,1)} %param.6, s32[]{:T(128)S(6)} %select_n.11, bf16[3072,64]{0,1:T(8,128)(2,1)S(1)} %all_gather.3), kind=kOutput, calls=%fused_computation.2 | convolution fusion | flops 3221225472 | bytes 54723584 | tf_op jit(solution)/shard_map/dot_general | solution.py:10
  30.1 89.5 %all-reduce.10 = bf16[16384,64]{0,1:T(8,128)(2,1)S(1)} all-reduce(f32[16384,64]{0,1:T(8,128)} %fusion.2), channel_id=1, replica_groups=mesh['row'=4,'col'=4,'depth'=2] {'row','depth'}, use_global_device_ids=true, to_apply=%region_0.0 | all-reduce | flops 1048576 | bytes 6291456 | tf_op jit(solution)/shard_map/psum | solution.py:46
  119.6 22.6 %fusion = f32[1536,64]{0,1:T(8,128)} fusion(bf16[3072,16384]{1,0:T(8,128)(2,1)} %param.6, s32[]{:T(128)S(6)} %select_n.11, bf16[16384,64]{0,1:T(8,128)(2,1)S(1)} %all-reduce.10), kind=kOutput, calls=%fused_computation | convolution fusion | flops 3221225472 | bytes 52822020 | tf_op jit(solution)/shard_map/dot_general | solution.py:50
  142.3 36.9 %all-reduce.5.cloned.1.call-done = f32[1536,64]{0,1:T(8,128)} async-done(((f32[1536,64]{0,1:T(8,128)}), f32[1536,64]{0,1:T(8,128)}) %all-reduce.5.cloned.1.call-update) | async-done | bytes 393232 | tf_op jit(solution)/shard_map/psum | solution.py:49
  179.2 7.6 %fusion.10 = f32[1024,64]{0,1:T(8,128)} fusion(f32[1536,64]{0,1:T(8,128)} %all-reduce.5.cloned.1.call-done, f32[3072,1024]{1,0:T(8,128)} %param.8, s32[]{:T(128)S(6)} %select_n.11), kind=kOutput, calls=%fused_computation.10 | convolution fusion | flops 1207959552 | bytes 6946820 | tf_op jit(solution)/shard_map/dot_general | solution.py:10
  187.0 53.1 %all-reduce.7.cloned.1.call-done = f32[1024,64]{0,1:T(8,128)} async-done(((f32[1024,64]{0,1:T(8,128)}), f32[1024,64]{0,1:T(8,128)}) %all-reduce.7.cloned.1.call-update) | async-done | bytes 262160 | tf_op jit(solution)/shard_map/psum | solution.py:54
  240.1 9.1 %fusion.12 = f32[1536,64]{0,1:T(8,128)S(1)} fusion(f32[1536,64]{0,1:T(8,128)} %all-reduce.5.cloned.1.call-done, f32[3072,1024]{1,0:T(8,128)} %param.8, s32[]{:T(128)S(6)} %select_n.11, f32[1024,64]{0,1:T(8,128)} %all-reduce.7.cloned.1.call-done), kind=kOutput, calls=%fused_computation.12 | convolution fusion | flops 1208123392 | bytes 7340036 | tf_op jit(solution)/shard_map/dot_general | solution.py:28
  249.6 22.4 %psum.45 = f32[64,64]{0,1:T(8,128)S(1)} all-reduce(f32[64,64]{0,1:T(8,128)S(1)} %fusion.56), channel_id=1, replica_groups=mesh['row'=4,'col'=4,'depth'=2] {'row','depth'}, use_global_device_ids=true, to_apply=%region_3.0 | all-reduce | flops 4096 | bytes 32768 | tf_op jit(solution)/shard_map/psum | solution.py:54
  272.1 5.8 %cholesky.44 = f32[64,64]{1,0:T(8,128)S(1)} custom-call(f32[64,64]{1,0:T(8,128)S(1)} %fusion.32), custom_call_target="Cholesky" | custom-call | tf_op jit(solution)/shard_map/jit(cholesky)/cholesky | solution.py:20
  278.6 0.7 select_bitcast_fusion.1
  279.3 4.9 %custom-call.6 = f32[1,64,64]{1,2,0:T(8,128)S(1)} custom-call(f32[1,64,64]{2,1,0:T(8,128)S(1)} %select_bitcast_fusion.1), custom_call_target="InvertDiagBlocksLowerTriangular" | custom-call | tf_op jit(solution)/shard_map/jit(_solve_triangular)/triangular_solve | solution.py:22
  284.9 7.6 %fusion.6 = f32[1024,64]{0,1:T(8,128)} fusion(f32[1536,64]{0,1:T(8,128)S(1)} %fusion.57, f32[3072,1024]{1,0:T(8,128)} %param.8, s32[]{:T(128)S(6)} %select_n.11), kind=kOutput, calls=%fused_computation.6 | convolution fusion | flops 1207959552 | bytes 6946820 | tf_op jit(solution)/shard_map/dot_general | solution.py:10
  292.5 53.0 %all-reduce.9.cloned.1.call-done = f32[1024,64]{0,1:T(8,128)} async-done(((f32[1024,64]{0,1:T(8,128)}), f32[1024,64]{0,1:T(8,128)}) %all-reduce.9.cloned.1.call-update) | async-done | bytes 262160 | tf_op jit(solution)/shard_map/psum | solution.py:54
  345.5 8.1 %fusion.15 = f32[1536,64]{0,1:T(8,128)S(1)} fusion(f32[1536,64]{0,1:T(8,128)S(1)} %fusion.57, f32[3072,1024]{1,0:T(8,128)} %param.8, s32[]{:T(128)S(6)} %select_n.11, f32[1024,64]{0,1:T(8,128)} %all-reduce.9.cloned.1.call-done), kind=kOutput, calls=%fused_computation.13 | convolution fusion | flops 1208123392 | bytes 7340036 | tf_op jit(solution)/shard_map/dot_general | solution.py:28
  354.1 22.4 %psum.47 = f32[64,64]{0,1:T(8,128)S(1)} all-reduce(f32[64,64]{0,1:T(8,128)S(1)} %fusion.58), channel_id=1, replica_groups=mesh['row'=4,'col'=4,'depth'=2] {'row','depth'}, use_global_device_ids=true, to_apply=%region_7.10 | all-reduce | flops 4096 | bytes 32768 | tf_op jit(solution)/shard_map/psum | solution.py:54
  376.6 5.8 %cholesky.55 = f32[64,64]{1,0:T(8,128)S(1)} custom-call(f32[64,64]{1,0:T(8,128)S(1)} %fusion.30), custom_call_target="Cholesky" | custom-call | tf_op jit(solution)/shard_map/jit(cholesky)/cholesky | solution.py:20
  383.1 2.1 fusion.34
  385.3 0.7 select_bitcast_fusion
  385.9 4.9 %custom-call.7 = f32[1,64,64]{1,2,0:T(8,128)S(1)} custom-call(f32[1,64,64]{2,1,0:T(8,128)S(1)} %select_bitcast_fusion), custom_call_target="InvertDiagBlocksLowerTriangular" | custom-call | tf_op jit(solution)/shard_map/jit(_solve_triangular)/triangular_solve | solution.py:22
  391.6 4.0 all_to_all.19
  395.6 0.8 copy.18
  396.4 2.0 fusion.19
  398.4 0.7 dynamic-slice_add_fusion
  (25 shorter events, 4.3 us)
Async XLA Ops:
  7.2 172.0 %all-reduce.5.cloned.1.call-start = ((), (), s32[]{:S(2)}) async-start(), calls=%async_computation.1 | async-start | bytes 786432 | tf_op jit(solution)/shard_map/psum | solution.py:49
  142.2 97.8 %all-reduce.7.cloned.1.call-start = ((), (), s32[]{:S(2)}) async-start(), calls=%async_computation.2 | async-start | bytes 524288 | tf_op jit(solution)/shard_map/psum | solution.py:54
  186.8 158.8 %all-reduce.9.cloned.1.call-start = ((), (), s32[]{:S(2)}) async-start(), calls=%async_computation.3 | async-start | bytes 524288 | tf_op jit(solution)/shard_map/psum | solution.py:54
  240.1 52.4 %copy-start = (f32[1024,64]{0,1:T(8,128)S(1)}, f32[1024,64]{0,1:T(8,128)}, u32[]{:S(2)}) copy-start(f32[1024,64]{0,1:T(8,128)} %all-reduce.7.cloned.1.call-done) | copy-start | bytes 786436
Sparse Core Ops, SparseCore 0:
  142.3 36.8 all-reduce.4
  186.9 53.1 all-reduce.6
  292.6 52.8 all-reduce.8
where the time goes:
time: 406 us
  waiting for transfers between devices  143 us (35%)
  blocking collectives  141 us (35%)
  matrix products  82 us (20%)
  other arithmetic  24.9 us (6%)
  between operations  13.9 us (3%)
    psum x2, waiting for transfers between devices, sum_layers(): return lax.psum(value, ('row', 'depth'))  106 us
    psum x1, blocking collectives, per_device(): lax.psum(contract_rows(panel_rows, start_rows, None), ('row', 'depth'))  89.5 us
    psum x2, blocking collectives, sum_layers(): return lax.psum(value, ('row', 'depth'))  44.7 us
    psum x1, waiting for transfers between devices, per_device(): lax.psum(jnp.dot(panel_rows, mixed_cols, preferred_element_type=jnp.float...  36.9 us
    dot_general x5, matrix products, contract_rows(): lax.dot_general(left_side, right_side, (((0,), (0,)), ((), ())), precisio...  36.5 us
    dot_general x1, matrix products, per_device(): jnp.dot(panel_rows, mixed_cols, preferred_element_type=jnp.float32)  22.6 us
    dot_general x2, matrix products, orthonormal_pass(): jnp.dot(stored_basis, projection, precision=HIGHEST, preferred_element_ty...  17.2 us
    another operation x6, other arithmetic, factor_gram(): lower_factor = jnp.linalg.cholesky(gram_matrix)  13 us
  transfers between devices with their start and end apart: 3, of which 3 were waited for; matrix products, arithmetic and copies ran while one was open for 0% of the time, Pallas kernels for 0%

commit v1 on v0

v1 whole, which is shorter than its diff:
```python
import functools

import jax
import jax.numpy as jnp
from jax import lax
from jax.experimental import pallas as pl
from jax.experimental.pallas import tpu as pltpu
from jax.sharding import PartitionSpec as P

HIGHEST = lax.Precision.HIGHEST
MESH = pl.DeviceIdType.MESH
F32 = jnp.float32
LANES = 128
LOOK = 4


def mm(a, b, precision=HIGHEST):
    return lax.dot_general(
        a, b, (((1,), (0,)), ((), ())), precision=precision, preferred_element_type=F32
    )


def mm_nt(a, b, precision=HIGHEST):
    return lax.dot_general(
        a, b, (((1,), (1,)), ((), ())), precision=precision, preferred_element_type=F32
    )


def factor(gram_twice):
    size = gram_twice.shape[0]
    rows = lax.broadcasted_iota(jnp.int32, (size, 2 * size), 0)
    lanes = lax.broadcasted_iota(jnp.int32, (size, 2 * size), 1)
    work = jnp.where(lanes < size, gram_twice, jnp.where(lanes - size == rows, 1.0, 0.0))

    def step(k, carry):
        work, pivots = carry
        at_lane = lanes == k
        at_row = rows == k
        column = jnp.sum(jnp.where(at_lane, work, 0.0), axis=1, keepdims=True)
        row = jnp.sum(jnp.where(at_row, work, 0.0), axis=0, keepdims=True)
        pivot_row = jnp.sum(jnp.where(at_lane & at_row, work, 0.0), axis=0, keepdims=True)
        pivot = jnp.sum(pivot_row, axis=1, keepdims=True)
        scale = column / pivot
        work = work - jnp.where(rows > k, scale * row, 0.0)
        pivots = jnp.where(at_row, pivot, pivots)
        return (work, pivots)

    work, pivots = lax.fori_loop(0, size, step, (work, jnp.ones_like(work)))
    work = work / jnp.sqrt(pivots)
    upper = jnp.where(rows <= lanes, work, 0.0)[:, :size]
    return (upper, work[:, size:])


def krylov_kernel(
    dims,
    panel_ref,
    start_ref,
    basis_ref,
    new_ref,
    coef_ref,
    tri_ref,
    held,
    start_all,
    part,
    gathered,
    image,
    sib_buf,
    col_buf,
    basis,
    proj_part,
    proj_in,
    proj_col,
    proj_all,
    gram_in,
    gram_col,
    out_part,
    out_buf,
    *rest,
):
    n_row, n_col, total_rows = dims
    stages = n_row.bit_length() - 1
    recvs = rest[:stages]
    (panel_sem, mix_send, mix_recv, misc_sem, sib_sem, col_send, col_recv,
     p_send, p_recv, z_send, z_recv, a_send, a_recv, g_send, g_recv, h_send, h_recv,
     o_send, o_recv) = rest[stages:]
    chunks, rows_here, width = held.shape
    cols = start_all.shape[0] * start_all.shape[1]
    pieces = image.shape[0]
    piece = image.shape[2]
    n_plane = n_row * 2
    row = lax.axis_index("row")
    col = lax.axis_index("col")
    core = lax.axis_index("depth")
    inv_total = 1.0 / total_rows

    def bit_of(value, bit):
        return (value // (1 << bit)) % 2

    def pick(first, second):
        return first * (1 - core) + second * core

    partners = []
    order = 0
    for s in range(stages):
        flips = [row + (1 - 2 * bit_of(row, b)) * (1 << b) for b in (s, stages - 1 - s)]
        partners.append(pick(flips[0], flips[1]))
        bits = pick(bit_of(row, s), bit_of(row, stages - 1 - s))
        order = order * 2 + bits
    plane_me = row * 2 + core
    col_group_me = core * n_col + col

    def plane_device(j):
        target = (plane_me + j) % n_plane
        return target, {"row": target // 2, "depth": target % 2}

    def col_device(j):
        target = (col + j) % n_col
        return target, {"col": target}

    def group_device(j):
        target = (col_group_me + j) % pieces
        return target, {"col": target % n_col, "depth": target // n_col}

    def panel_copy(t):
        first = pl.multiple_of((core * chunks + t) * width, width)
        return pltpu.make_async_copy(
            panel_ref.at[:, pl.ds(first, width)], held.at[t], panel_sem.at[t]
        )

    for t in range(min(LOOK, chunks)):
        panel_copy(t).start()

    basis_first = pl.multiple_of(col_group_me * piece, 8)
    basis_copy = pltpu.make_async_copy(
        basis_ref.at[pl.ds(basis_first, piece), :], basis, misc_sem.at[0]
    )
    own_start = pltpu.make_async_copy(start_ref, start_all.at[core], misc_sem.at[1])
    own_start.start()

    barrier = pltpu.get_barrier_semaphore()
    greeted = 0
    for j in range(1, n_plane):
        pl.semaphore_signal(barrier, inc=1, device_id=plane_device(j)[1], device_id_type=MESH)
        greeted += 1
    for j in range(1, pieces):
        pl.semaphore_signal(barrier, inc=1, device_id=group_device(j)[1], device_id_type=MESH)
        greeted += 1
    pl.semaphore_wait(barrier, greeted)

    def remote(src, dst, send_sem, recv_sem, device):
        return pltpu.make_async_remote_copy(
            src_ref=src,
            dst_ref=dst,
            send_sem=send_sem,
            recv_sem=recv_sem,
            device_id=device,
            device_id_type=MESH,
        )

    sibling = {"depth": 1 - core}
    start_copy = remote(start_ref, start_all.at[core], sib_sem.at[0], sib_sem.at[1], sibling)
    start_copy.start()
    image[...] = jnp.zeros_like(image)
    own_start.wait()
    start_copy.wait()

    def span(s):
        length = n_row >> s
        return (order // length) * length, length

    def reduce_copy(s, t):
        first, length = span(s)
        half = length // 2
        mine = span(s + 1)[0]
        other = first + (first + half - mine)
        return remote(
            part.at[t, pl.ds(other, half)],
            recvs[s].at[t],
            mix_send.at[s, t],
            mix_recv.at[s, t],
            {"row": partners[s]},
        )

    def gather_copy(s, t):
        level = stages - 1 - s
        first, length = span(level + 1)
        region = gathered.at[t, pl.ds(first, length)]
        return remote(
            region, region, mix_send.at[stages + s, t], mix_recv.at[stages + s, t],
            {"row": partners[level]},
        )

    block = rows_here // 4
    per_block = block // piece

    def body(i, carry):
        for s in reversed(range(stages)):
            t = i - (stages + 1 + s)

            if s < stages - 1:
                @pl.when((t >= 0) & (t < chunks))
                def _():
                    gather_copy(s, t).wait_recv()
                    gather_copy(s + 1, t).start()

        for s in reversed(range(stages)):
            t = i - (s + 1)

            @pl.when((t >= 0) & (t < chunks))
            def _():
                reduce_copy(s, t).wait_recv()
                first, length = span(s + 1)
                summed = part[t, pl.ds(first, length)] + recvs[s][t]
                if s < stages - 1:
                    part[t, pl.ds(first, length)] = summed
                    reduce_copy(s + 1, t).start()
                else:
                    gathered[t, pl.ds(first, length)] = summed.astype(jnp.bfloat16)
                    gather_copy(0, t).start()

        @pl.when(i < chunks)
        def _():
            @pl.when(i + LOOK < chunks)
            def _():
                panel_copy(i + LOOK).start()

            panel_copy(i).wait()
            lhs = start_all[...].reshape(cols, rows_here)
            mixed = mm(lhs, held[i], None)
            for p in range(n_row):
                part[i, p] = mixed[:, p * LANES : (p + 1) * LANES]
            reduce_copy(0, i).start()

        t = i - 2 * stages

        @pl.when(t >= 0)
        def _():
            gather_copy(stages - 1, t).wait_recv()
            lhs = jnp.concatenate([gathered[t, p] for p in range(n_row)], axis=1)
            for h in range(4):
                got = mm_nt(lhs, held[t, h * block : (h + 1) * block, :], None)
                for q in range(per_block):
                    image[h * per_block + q] += got[:, q * piece : (q + 1) * piece]

        return carry

    lax.fori_loop(0, chunks + 2 * stages, body, 0)
    basis_copy.start()

    half_copy = remote(
        image.at[pl.ds((1 - core) * n_col, n_col)], sib_buf, sib_sem.at[2], sib_sem.at[3], sibling
    )
    half_copy.start()
    half_copy.wait()
    sib_buf[...] = sib_buf[...] + image[pl.ds(core * n_col, n_col)]
    copies = []
    for j in range(1, n_col):
        target, device = col_device(j)
        copies.append(
            remote(sib_buf.at[target], col_buf.at[col], col_send.at[j], col_recv.at[j], device)
        )
        copies[-1].start()
    col_buf[col] = sib_buf[col]

    def drain(t, carry):
        for s in range(stages):
            reduce_copy(s, t).wait_send()
            gather_copy(s, t).wait_send()
        return carry

    lax.fori_loop(0, chunks, drain, 0)
    basis_copy.wait()
    for copy in copies:
        copy.wait()

    image_t = col_buf[0]
    for c in range(1, n_col):
        image_t = image_t + col_buf[c]

    k_total = basis.shape[1]
    piece_rows, piece_lanes = proj_part.shape[1:]
    lane_blocks = k_total // piece_lanes

    def start_plane(slot, src_of, dst, send, recv):
        made = []
        for j in range(1, n_plane):
            target, device = plane_device(j)
            made.append(remote(src_of(target), dst, send.at[slot, j], recv.at[slot, j], device))
            made[-1].start()
        return made

    def start_cols(slot, src, dst, send, recv):
        made = []
        for j in range(1, n_col):
            target, device = col_device(j)
            made.append(remote(src, dst, send.at[slot, j], recv.at[slot, j], device))
            made[-1].start()
        return made

    def finish(made):
        for copy in made:
            copy.wait()

    def ordered_sum(ref, slot, count):
        total = ref[slot, 0]
        for c in range(1, count):
            total = total + ref[slot, c]
        return total

    def project_start(slot, value):
        for p in range(n_plane):
            lane = (p % lane_blocks) * piece_lanes
            top = (p // lane_blocks) * piece_rows
            proj_part[p] = value[top : top + piece_rows, lane : lane + piece_lanes]
        copies = start_plane(
            slot, lambda target: proj_part.at[target], proj_in.at[slot, plane_me], p_send, p_recv
        )
        proj_in[slot, plane_me] = proj_part[plane_me]
        return copies

    def project_mid(slot, copies):
        finish(copies)
        proj_col[slot, col] = ordered_sum(proj_in, slot, n_plane)
        mine = proj_col.at[slot, col]
        return start_cols(slot, mine, mine, z_send, z_recv)

    def project_end(slot, copies):
        finish(copies)
        proj_all[slot, plane_me] = ordered_sum(proj_col, slot, n_col) * inv_total
        mine = proj_all.at[slot, plane_me]
        return start_plane(slot, lambda target: mine, mine, a_send, a_recv)

    def project_value(slot):
        bands = []
        for top in range(n_plane // lane_blocks):
            bands.append(
                jnp.concatenate(
                    [proj_all[slot, top * lane_blocks + p] for p in range(lane_blocks)], axis=1
                )
            )
        return jnp.concatenate(bands, axis=0) if len(bands) > 1 else bands[0]

    def gram_start(slot, value):
        gram_in[slot, plane_me] = mm_nt(value, jnp.concatenate([value, value], axis=0))
        mine = gram_in.at[slot, plane_me]
        return start_plane(slot, lambda target: mine, mine, g_send, g_recv)

    def gram_mid(slot, copies):
        finish(copies)
        gram_col[slot, col] = ordered_sum(gram_in, slot, n_plane)
        mine = gram_col.at[slot, col]
        return start_cols(slot, mine, mine, h_send, h_recv)

    def gram_end(slot, copies):
        finish(copies)
        return ordered_sum(gram_col, slot, n_col) * inv_total

    copies = project_start(0, mm(image_t, basis[...]))
    copies = project_mid(0, copies)
    finish(project_end(0, copies))
    proj_first = project_value(0)
    remainder = image_t - mm_nt(proj_first, basis[...])

    gram_copies = gram_start(0, remainder)
    copies = project_start(1, mm(remainder, basis[...]))
    gram_copies = gram_mid(0, gram_copies)
    copies = project_mid(1, copies)
    gram_first = gram_end(0, gram_copies)
    copies = project_end(1, copies)
    upper_first, inverse_first = factor(gram_first)
    finish(copies)
    proj_second = project_value(1)
    coef = proj_first + proj_second
    half = coef_ref.shape[0]
    proj_second_rem = remainder - mm_nt(proj_second, basis[...])
    second = mm(inverse_first, proj_second_rem)

    gram_copies = gram_start(1, second)

    @pl.when(core == 0)
    def _():
        coef_ref[...] = coef[:half]

    @pl.when(core == 1)
    def _():
        coef_ref[...] = coef[half:]

    gram_copies = gram_mid(1, gram_copies)
    gram_second = gram_end(1, gram_copies)
    upper_second, inverse_second = factor(gram_second)
    new_t = mm(inverse_second, second)
    out_part[0] = new_t[:half]
    out_part[1] = new_t[half:]
    copies = []
    for j in range(1, pieces):
        target, device = group_device(j)
        copies.append(
            remote(
                out_part.at[target // n_col], out_buf.at[col_group_me],
                o_send.at[j], o_recv.at[j], device,
            )
        )
        copies[-1].start()
    out_buf[col_group_me] = out_part[core]
    tri_ref[...] = mm(upper_second, upper_first)
    finish(copies)
    for q in range(pieces):
        new_ref[:, q * piece : (q + 1) * piece] = out_buf[q]


def per_device(matrix_panel, start_block, stored_basis):
    n_row = lax.axis_size("row")
    n_col = lax.axis_size("col")
    n_core = lax.axis_size("depth")
    rows_here, cols_here = matrix_panel.shape
    half = start_block.shape[1]
    cols = half * n_core
    k_total = stored_basis.shape[1]
    stages = n_row.bit_length() - 1
    width = LANES * n_row
    chunks = cols_here // n_core // width
    pieces = n_col * n_core
    piece = rows_here // pieces
    n_plane = n_row * n_core
    piece_lanes = max(LANES, k_total // n_plane)
    piece_rows = cols * k_total // (n_plane * piece_lanes)
    dma = pltpu.SemaphoreType.DMA
    scratch = [
        pltpu.VMEM((chunks, rows_here, width), jnp.bfloat16),
        pltpu.VMEM((n_core, half, rows_here), jnp.bfloat16),
        pltpu.VMEM((chunks, n_row, cols, LANES), F32),
        pltpu.VMEM((chunks, n_row, cols, LANES), jnp.bfloat16),
        pltpu.VMEM((pieces, cols, piece), F32),
        pltpu.VMEM((n_col, cols, piece), F32),
        pltpu.VMEM((n_col, cols, piece), F32),
        pltpu.VMEM((piece, k_total), F32),
        pltpu.VMEM((n_plane, piece_rows, piece_lanes), F32),
        pltpu.VMEM((2, n_plane, piece_rows, piece_lanes), F32),
        pltpu.VMEM((2, n_col, piece_rows, piece_lanes), F32),
        pltpu.VMEM((2, n_plane, piece_rows, piece_lanes), F32),
        pltpu.VMEM((2, n_plane, cols, 2 * cols), F32),
        pltpu.VMEM((2, n_col, cols, 2 * cols), F32),
        pltpu.VMEM((n_core, half, piece), F32),
        pltpu.VMEM((pieces, half, piece), F32),
    ]
    scratch += [
        pltpu.VMEM((chunks, n_row >> (s + 1), cols, LANES), F32) for s in range(stages)
    ]
    scratch += [
        dma((chunks,)),
        dma((2 * stages, chunks)),
        dma((2 * stages, chunks)),
        dma((2,)),
        dma((4,)),
        dma((n_col,)),
        dma((n_col,)),
        dma((2, n_plane)),
        dma((2, n_plane)),
        dma((2, n_col)),
        dma((2, n_col)),
        dma((2, n_plane)),
        dma((2, n_plane)),
        dma((2, n_plane)),
        dma((2, n_plane)),
        dma((2, n_col)),
        dma((2, n_col)),
        dma((pieces,)),
        dma((pieces,)),
    ]
    whole = pl.BlockSpec(memory_space=pltpu.VMEM)
    hbm = pl.BlockSpec(memory_space=pl.ANY)
    new_t, coef_t, triangle = pl.pallas_call(
        functools.partial(krylov_kernel, (n_row, n_col, rows_here * n_row)),
        out_shape=(
            jax.ShapeDtypeStruct((half, rows_here), F32),
            jax.ShapeDtypeStruct((half, k_total), F32),
            jax.ShapeDtypeStruct((cols, cols), F32),
        ),
        in_specs=[hbm, whole, hbm],
        out_specs=(whole, whole, whole),
        scratch_shapes=scratch,
        compiler_params=pltpu.CompilerParams(
            collective_id=0, has_side_effects=True, vmem_limit_bytes=63 << 20
        ),
    )(matrix_panel, start_block.T, stored_basis)
    return (new_t.T, coef_t.T, triangle)


def solution(mesh):
    placed = (P("row", "col"), P("row", "depth"), P("row", None))
    return jax.shard_map(
        per_device,
        mesh=mesh,
        in_specs=placed,
        out_specs=(P("row", "depth"), P(None, "depth"), P()),
        check_vma=False,
    )
```

time: 406 us -> 167 us (0.41)
  Pallas kernels: 0 us -> 161 us
  waiting for transfers between devices: 143 us -> 0 us
  blocking collectives: 141 us -> 0 us
  matrix products: 82 us -> 0 us
  other arithmetic: 24.9 us -> 0 us
  between operations: 13.9 us -> 0.64 us
    pallas_call x0 -> x1, Pallas kernels: none -> 161 us  [per_device(): pl.pallas_call(functools.partial(krylov_kernel, (n_row, n_col, rows_here...]
    psum x3 -> x0, waiting for transfers between devices: 143 us -> none  [the longest x2 106 us: sum_layers(): return lax.psum(value, ('row', 'depth'))]
    psum x3 -> x0, blocking collectives: 134 us -> none  [the longest x1 89.5 us: per_device(): lax.psum(contract_rows(panel_rows, start_rows, None), ('row', 'depth'))]
    dot_general x12 -> x0, matrix products: 81.5 us -> none  [the longest x5 36.5 us: contract_rows(): lax.dot_general(left_side, right_side, (((0,), (0,)), ((), ())), precisio...]
    another operation x10 -> x0, other arithmetic: 24.1 us -> none  [the longest x6 13 us: factor_gram(): lower_factor = jnp.linalg.cholesky(gram_matrix)]
    unnamed x2 -> x3, local copies, waits for them, and re-layouts: 0.01 us -> 4.71 us
  transfers between devices with their start and end apart: 3 -> 0, of which waited for: 3 -> 0; matrix products, arithmetic and copies ran while one was open for 0% -> 0% of each run, Pallas kernels for 0% -> 0%
where the time goes in v1:
time: 167 us
  Pallas kernels  161 us (96%)
  local copies, waits for them, and re-layouts  4.71 us (3%)
    pallas_call x1, Pallas kernels, per_device(): pl.pallas_call(functools.partial(krylov_kernel, (n_row, n_col, rows_here...  161 us
    unnamed x3, local copies, waits for them, and re-layouts  4.71 us

profile of v1, /device:TPU:0, one launch (start us, length us, event | category | flops | bytes accessed | tf_op | source)
XLA Modules:
  0.0 166.8 jit_solution(12301994883053047557)
XLA Ops:
  0.6 161.4 %shard_map.58 = (f32[32,3072]{1,0:T(8,128)}, f32[32,1024]{1,0:T(8,128)}, f32[64,64]{1,0:T(8,128)}) custom-call(bf16[3072,16384]{1,0:T(8,128)(2,1)} %panel_ref.1, bf16[32,3072]{1,0:T(8,128)(2,1)} %bitcast.4, f32[3072,1024]{1,0:T(8,128)} %basis_ref.1), custom_call_target="tpu_custom_call" | custom-call | tf_op jit(solution)/shard_map/pallas_call | solution.py:472
  162.1 1.8 %copy.9 = f32[3072,32]{0,1:T(8,128)} copy(f32[3072,32]{0,1:T(8,128)} %bitcast.3) | data formatting | bytes 786432
  163.8 1.6 copy.10
  165.4 1.4 copy.11

commit v2 on v1

--- a/solution.py
+++ b/solution.py
@@ -12,6 +12,7 @@
 F32 = jnp.float32
 LANES = 128
 LOOK = 4
+LAG = 3
 
 
 def mm(a, b, precision=HIGHEST):
@@ -32,20 +33,35 @@
     lanes = lax.broadcasted_iota(jnp.int32, (size, 2 * size), 1)
     work = jnp.where(lanes < size, gram_twice, jnp.where(lanes - size == rows, 1.0, 0.0))
 
-    def step(k, carry):
+    def all_sum(mask, value):
+        part_sum = jnp.sum(jnp.where(mask, value, 0.0), axis=0, keepdims=True)
+        return jnp.sum(part_sum, axis=1, keepdims=True)
+
+    def step(i, carry):
         work, pivots = carry
-        at_lane = lanes == k
-        at_row = rows == k
-        column = jnp.sum(jnp.where(at_lane, work, 0.0), axis=1, keepdims=True)
-        row = jnp.sum(jnp.where(at_row, work, 0.0), axis=0, keepdims=True)
-        pivot_row = jnp.sum(jnp.where(at_lane & at_row, work, 0.0), axis=0, keepdims=True)
-        pivot = jnp.sum(pivot_row, axis=1, keepdims=True)
-        scale = column / pivot
-        work = work - jnp.where(rows > k, scale * row, 0.0)
-        pivots = jnp.where(at_row, pivot, pivots)
+        k = 2 * i
+        n = k + 1
+        lane_k, lane_n = lanes == k, lanes == n
+        row_is_k, row_is_n = rows == k, rows == n
+        column_k = jnp.sum(jnp.where(lane_k, work, 0.0), axis=1, keepdims=True)
+        column_n = jnp.sum(jnp.where(lane_n, work, 0.0), axis=1, keepdims=True)
+        row_k = jnp.sum(jnp.where(row_is_k, work, 0.0), axis=0, keepdims=True)
+        row_n = jnp.sum(jnp.where(row_is_n, work, 0.0), axis=0, keepdims=True)
+        pivot_k = all_sum(row_is_k & lane_k, work)
+        upper = all_sum(row_is_k & lane_n, work)
+        lower = all_sum(row_is_n & lane_k, work)
+        corner = all_sum(row_is_n & lane_n, work)
+        ratio = lower / pivot_k
+        pivot_n = corner - ratio * upper
+        row_n = row_n - ratio * row_k
+        scale_k = column_k / pivot_k
+        scale_n = (column_n - scale_k * upper) / pivot_n
+        work = work - jnp.where(rows > k, scale_k * row_k, 0.0)
+        work = work - jnp.where(rows > n, scale_n * row_n, 0.0)
+        pivots = jnp.where(row_is_k, pivot_k, jnp.where(row_is_n, pivot_n, pivots))
         return (work, pivots)
 
-    work, pivots = lax.fori_loop(0, size, step, (work, jnp.ones_like(work)))
+    work, pivots = lax.fori_loop(0, size // 2, step, (work, jnp.ones_like(work)))
     work = work / jnp.sqrt(pivots)
     upper = jnp.where(rows <= lanes, work, 0.0)[:, :size]
     return (upper, work[:, size:])
@@ -75,6 +91,7 @@
     gram_col,
     out_part,
     out_buf,
+    second_all,
     *rest,
 ):
     n_row, n_col, total_rows = dims
@@ -82,7 +99,7 @@
     recvs = rest[:stages]
     (panel_sem, mix_send, mix_recv, misc_sem, sib_sem, col_send, col_recv,
      p_send, p_recv, z_send, z_recv, a_send, a_recv, g_send, g_recv, h_send, h_recv,
-     o_send, o_recv) = rest[stages:]
+     o_send, o_recv, half_send, half_recv, s_send, s_recv) = rest[stages:]
     chunks, rows_here, width = held.shape
     cols = start_all.shape[0] * start_all.shape[1]
     pieces = image.shape[0]
@@ -117,10 +134,6 @@
         target = (col + j) % n_col
         return target, {"col": target}
 
-    def group_device(j):
-        target = (col_group_me + j) % pieces
-        return target, {"col": target % n_col, "depth": target // n_col}
-
     def panel_copy(t):
         first = pl.multiple_of((core * chunks + t) * width, width)
         return pltpu.make_async_copy(
@@ -142,8 +155,8 @@
     for j in range(1, n_plane):
         pl.semaphore_signal(barrier, inc=1, device_id=plane_device(j)[1], device_id_type=MESH)
         greeted += 1
-    for j in range(1, pieces):
-        pl.semaphore_signal(barrier, inc=1, device_id=group_device(j)[1], device_id_type=MESH)
+    for j in range(1, n_col):
+        pl.semaphore_signal(barrier, inc=1, device_id=col_device(j)[1], device_id_type=MESH)
         greeted += 1
     pl.semaphore_wait(barrier, greeted)
 
@@ -195,7 +208,7 @@
 
     def body(i, carry):
         for s in reversed(range(stages)):
-            t = i - (stages + 1 + s)
+            t = i - LAG * (stages + 1 + s)
 
             if s < stages - 1:
                 @pl.when((t >= 0) & (t < chunks))
@@ -204,7 +217,7 @@
                     gather_copy(s + 1, t).start()
 
         for s in reversed(range(stages)):
-            t = i - (s + 1)
+            t = i - LAG * (s + 1)
 
             @pl.when((t >= 0) & (t < chunks))
             def _():
@@ -231,7 +244,7 @@
                 part[i, p] = mixed[:, p * LANES : (p + 1) * LANES]
             reduce_copy(0, i).start()
 
-        t = i - 2 * stages
+        t = i - LAG * 2 * stages
 
         @pl.when(t >= 0)
         def _():
@@ -244,23 +257,27 @@
 
         return carry
 
-    lax.fori_loop(0, chunks + 2 * stages, body, 0)
+    lax.fori_loop(0, chunks + LAG * 2 * stages, body, 0)
     basis_copy.start()
 
-    half_copy = remote(
-        image.at[pl.ds((1 - core) * n_col, n_col)], sib_buf, sib_sem.at[2], sib_sem.at[3], sibling
-    )
-    half_copy.start()
-    half_copy.wait()
-    sib_buf[...] = sib_buf[...] + image[pl.ds(core * n_col, n_col)]
+    def half_copy(c):
+        return remote(
+            image.at[(1 - core) * n_col + c], sib_buf.at[c], half_send.at[c], half_recv.at[c], sibling
+        )
+
+    for j in range(1, n_col + 1):
+        half_copy((col + j) % n_col).start()
     copies = []
     for j in range(1, n_col):
         target, device = col_device(j)
+        half_copy(target).wait_recv()
+        sib_buf[target] = sib_buf[target] + image[core * n_col + target]
         copies.append(
             remote(sib_buf.at[target], col_buf.at[col], col_send.at[j], col_recv.at[j], device)
         )
         copies[-1].start()
-    col_buf[col] = sib_buf[col]
+    half_copy(col).wait_recv()
+    col_buf[col] = sib_buf[col] + image[core * n_col + col]
 
     def drain(t, carry):
         for s in range(stages):
@@ -269,6 +286,8 @@
         return carry
 
     lax.fori_loop(0, chunks, drain, 0)
+    for c in range(n_col):
+        half_copy(c).wait_send()
     basis_copy.wait()
     for copy in copies:
         copy.wait()
@@ -341,19 +360,19 @@
         return jnp.concatenate(bands, axis=0) if len(bands) > 1 else bands[0]
 
     def gram_start(slot, value):
-        gram_in[slot, plane_me] = mm_nt(value, jnp.concatenate([value, value], axis=0))
+        gram_col[slot, col] = mm_nt(value, jnp.concatenate([value, value], axis=0))
+        mine = gram_col.at[slot, col]
+        return start_cols(slot, mine, mine, h_send, h_recv)
+
+    def gram_mid(slot, copies):
+        finish(copies)
+        gram_in[slot, plane_me] = ordered_sum(gram_col, slot, n_col)
         mine = gram_in.at[slot, plane_me]
         return start_plane(slot, lambda target: mine, mine, g_send, g_recv)
 
-    def gram_mid(slot, copies):
-        finish(copies)
-        gram_col[slot, col] = ordered_sum(gram_in, slot, n_plane)
-        mine = gram_col.at[slot, col]
-        return start_cols(slot, mine, mine, h_send, h_recv)
-
     def gram_end(slot, copies):
         finish(copies)
-        return ordered_sum(gram_col, slot, n_col) * inv_total
+        return ordered_sum(gram_in, slot, n_plane) * inv_total
 
     copies = project_start(0, mm(image_t, basis[...]))
     copies = project_mid(0, copies)
@@ -376,6 +395,13 @@
     second = mm(inverse_first, proj_second_rem)
 
     gram_copies = gram_start(1, second)
+    second_all[col] = second
+    second_copies = []
+    for j in range(1, n_col):
+        target, device = col_device(j)
+        mine = second_all.at[col]
+        second_copies.append(remote(mine, mine, s_send.at[j], s_recv.at[j], device))
+        second_copies[-1].start()
 
     @pl.when(core == 0)
     def _():
@@ -388,20 +414,21 @@
     gram_copies = gram_mid(1, gram_copies)
     gram_second = gram_end(1, gram_copies)
     upper_second, inverse_second = factor(gram_second)
-    new_t = mm(inverse_second, second)
-    out_part[0] = new_t[:half]
-    out_part[1] = new_t[half:]
+    finish(second_copies)
     copies = []
-    for j in range(1, pieces):
-        target, device = group_device(j)
+    for c in range(n_col):
+        new_t = mm(inverse_second, second_all[c])
+        out_part[c, 0] = new_t[:half]
+        out_part[c, 1] = new_t[half:]
         copies.append(
             remote(
-                out_part.at[target // n_col], out_buf.at[col_group_me],
-                o_send.at[j], o_recv.at[j], device,
+                out_part.at[c, 1 - core], out_buf.at[core * n_col + c],
+                o_send.at[c], o_recv.at[c], sibling,
             )
         )
         copies[-1].start()
-    out_buf[col_group_me] = out_part[core]
+    for c in range(n_col):
+        out_buf[core * n_col + c] = out_part[c, core]
     tri_ref[...] = mm(upper_second, upper_first)
     finish(copies)
     for q in range(pieces):
@@ -440,8 +467,9 @@
         pltpu.VMEM((2, n_plane, piece_rows, piece_lanes), F32),
         pltpu.VMEM((2, n_plane, cols, 2 * cols), F32),
         pltpu.VMEM((2, n_col, cols, 2 * cols), F32),
-        pltpu.VMEM((n_core, half, piece), F32),
+        pltpu.VMEM((n_col, n_core, half, piece), F32),
         pltpu.VMEM((pieces, half, piece), F32),
+        pltpu.VMEM((n_col, cols, piece), F32),
     ]
     scratch += [
         pltpu.VMEM((chunks, n_row >> (s + 1), cols, LANES), F32) for s in range(stages)
@@ -451,7 +479,7 @@
         dma((2 * stages, chunks)),
         dma((2 * stages, chunks)),
         dma((2,)),
-        dma((4,)),
+        dma((2,)),
         dma((n_col,)),
         dma((n_col,)),
         dma((2, n_plane)),
@@ -464,8 +492,12 @@
         dma((2, n_plane)),
         dma((2, n_col)),
         dma((2, n_col)),
-        dma((pieces,)),
-        dma((pieces,)),
+        dma((n_col,)),
+        dma((n_col,)),
+        dma((n_col,)),
+        dma((n_col,)),
+        dma((n_col,)),
+        dma((n_col,)),
     ]
     whole = pl.BlockSpec(memory_space=pltpu.VMEM)
     hbm = pl.BlockSpec(memory_space=pl.ANY)

time: 167 us -> 118 us (0.71)
  Pallas kernels: 161 us -> 113 us
    pallas_call x1, Pallas kernels: 161 us -> 113 us  [per_device(): pl.pallas_call(functools.partial(krylov_kernel, (n_row, n_col, rows_here...]
where the time goes in v2:
time: 118 us
  Pallas kernels  113 us (96%)
  local copies, waits for them, and re-layouts  4.71 us (4%)
    pallas_call x1, Pallas kernels, per_device(): pl.pallas_call(functools.partial(krylov_kernel, (n_row, n_col, rows_here...  113 us
    unnamed x3, local copies, waits for them, and re-layouts  4.71 us

profile of v2, /device:TPU:0, one launch (start us, length us, event | category | flops | bytes accessed | tf_op | source)
XLA Modules:
  0.0 118.2 jit_solution(8825080619077749485)
XLA Ops:
  0.6 112.8 %shard_map.58 = (f32[32,3072]{1,0:T(8,128)}, f32[32,1024]{1,0:T(8,128)}, f32[64,64]{1,0:T(8,128)}) custom-call(bf16[3072,16384]{1,0:T(8,128)(2,1)} %panel_ref.1, bf16[32,3072]{1,0:T(8,128)(2,1)} %bitcast.4, f32[3072,1024]{1,0:T(8,128)} %basis_ref.1), custom_call_target="tpu_custom_call" | custom-call | tf_op jit(solution)/shard_map/pallas_call | solution.py:504
  113.4 1.8 %copy.9 = f32[3072,32]{0,1:T(8,128)} copy(f32[3072,32]{0,1:T(8,128)} %bitcast.3) | data formatting | bytes 786432
  115.2 1.6 %copy.10 = f32[1024,32]{0,1:T(8,128)} copy(f32[1024,32]{0,1:T(8,128)} %bitcast.5) | data formatting | bytes 262144
  116.8 1.4 %copy.11 = f32[64,64]{1,0:T(8,128)} copy(f32[64,64]{1,0:T(8,128)} %get-tuple-element.14) | data formatting | bytes 32768
